TPU v7x, 256 devices: a whole 4x4x8 slice. The times are simulated.
256 devices in a mesh: gx: 16 (over z, x_hi), gy: 16 (over x_lo, y, core).
Axes of the slice: x: 4 (x_hi: 2, x_lo: 2; x = x_hi * 2 + x_lo), y: 4, z: 8, core: 2. Of those that a mesh axis runs over, the one named last changes fastest.
Arguments:
- tokens: bfloat16 [4096, 4096], P('gy', 'gx'), may hold values from -6 to 6
- attn_gain: bfloat16 [4096], replicated, may hold values from 0.099609375 to 1.8984375
- qkv_weight: bfloat16 [4096, 6144], P('gy', 'gx'), may hold values from -0.1875 to 0.1875
- out_weight: bfloat16 [4096, 4096], P('gx', 'gy'), may hold values from -0.09375 to 0.09375
- mlp_gain: bfloat16 [4096], replicated, may hold values from 0.099609375 to 1.8984375
- up_weight: bfloat16 [4096, 12288], P('gy', 'gx'), may hold values from -0.09375 to 0.09375
- down_weight: bfloat16 [12288, 4096], P('gx', 'gy'), may hold values from -0.0546875 to 0.0546875
- final_gain: bfloat16 [4096], replicated, may hold values from 0.099609375 to 1.8984375
- head_weight: bfloat16 [4096, 131072], P(None, ('gx', 'gy')), may hold values from -0.25 to 0.25
- kv_cache: bfloat16 [256, 4096, 256], P(('gy', 'gx')), may hold values from -40 to 40
- cache_lengths: int32 [32], replicated, may hold values from 1 to 3968, as said below
- slot_request: int32 [32], replicated, may hold values from 0 to 31, each once
Outputs:
- hidden_out: bfloat16 [4096, 4096], P('gy', 'gx')
- new_cache: bfloat16 [256, 4096, 256], P(('gy', 'gx'))
- last_norms: float32 [32], replicated
- max_logits: float32 [32], replicated
- head_input: bfloat16 [32, 4096], replicated
Inputs may be any that keep to these rules, and one draw needn't show every extreme that they name: `cache_lengths`: the longest request has exactly 3968 cached positions.
All inputs are finite; a program needn't handle non-finite values.
Results may differ from a plain program's by a relative error of at most 0.02.
The roundings to bfloat16 on the way count: a program that leaves them out, or rounds other values in their place, can miss the bound.
Values may be sent and summed in bfloat16 or wider, within the bound.
A program may use at most 128 MiB of HBM per device.

v0:
```python
import math

import jax
import jax.numpy as jnp
from jax import lax
from jax.sharding import PartitionSpec as P

HEADS = 32
KVH = 8
HD = 128


epsilon = 1e-05
negative = -1e30


def from_partner(block, axis, distance):
    count = lax.axis_size(axis)
    route = []
    for low in range(count):
        high = low | 1 << distance
        if high != low and high < count:
            route += [(low, high), (high, low)]
    return lax.ppermute(block, axis, route)


def rms_factor(row_block):
    return lax.rsqrt(jnp.mean(row_block * row_block, axis=-1, keepdims=True) + epsilon)


def gather_features(shard_rows):
    return lax.all_gather(shard_rows, "gx", axis=1, tiled=True)


def rows_product(left_rows, weight_shard):
    return jnp.dot(
        left_rows,
        lax.all_gather(weight_shard, "gy", axis=0, tiled=True),
        preferred_element_type=jnp.float32,
    )


def columns_product(left_rows, weight_shard):
    return jnp.dot(
        left_rows,
        lax.all_gather(weight_shard, "gy", axis=1, tiled=True),
        preferred_element_type=jnp.float32,
    )


def pair_swap(values):
    return from_partner(values, "gx", KVH.bit_length() - 1)


def scatter_partials(partial_terms):
    return lax.psum_scatter(
        partial_terms.astype(jnp.bfloat16), "gx", scatter_dimension=1, tiled=True
    ).astype(jnp.float32)


def merge_block(carried, scores, value_rows):
    row_max, running, numerator = carried
    new_max = jnp.maximum(row_max, jnp.max(scores, axis=1, keepdims=True))
    factor = jnp.exp(row_max - new_max)
    weights = jnp.exp(scores - new_max)
    running = running * factor + jnp.sum(weights, axis=1, keepdims=True)
    numerator = numerator * factor + jnp.dot(
        weights.astype(jnp.bfloat16), value_rows, preferred_element_type=jnp.float32
    )
    return (new_max, running, numerator)


def attend_cache(group_cols, cache_rows, length, new_rows):
    per_group = HEADS // KVH
    scaling = 1.0 / math.sqrt(HD)
    query_rows = per_group * new_rows
    queries = (
        group_cols[:, : per_group * HD]
        .reshape(new_rows, per_group, HD)
        .transpose(1, 0, 2)
        .reshape(query_rows, HD)
    )
    key_new = group_cols[:, per_group * HD : (per_group + 1) * HD]
    value_new = group_cols[:, (per_group + 1) * HD :]
    block_len = min(512, cache_rows.shape[0])

    def visit_block(step_index, carried):
        offset = step_index * block_len
        block_rows = lax.dynamic_slice_in_dim(cache_rows, offset, block_len, 0)
        scores = (
            jnp.dot(queries, block_rows[:, :HD].T, preferred_element_type=jnp.float32) * scaling
        )
        positions = offset + jnp.arange(block_len)
        scores = jnp.where(positions[None, :] < length, scores, negative)
        return merge_block(carried, scores, block_rows[:, HD:])

    initial = (
        jnp.full((query_rows, 1), negative, jnp.float32),
        jnp.zeros((query_rows, 1), jnp.float32),
        jnp.zeros((query_rows, HD), jnp.float32),
    )
    block_count = (length + block_len - 1) // block_len
    carried = lax.fori_loop(0, block_count, visit_block, initial)
    new_scores = jnp.dot(queries, key_new.T, preferred_element_type=jnp.float32) * scaling
    causal = jnp.arange(new_rows)[None, :] <= (jnp.arange(query_rows) % new_rows)[:, None]
    new_scores = jnp.where(causal, new_scores, negative)
    row_max, running, numerator = merge_block(carried, new_scores, value_new)
    attended = (numerator / running).astype(jnp.bfloat16)
    attended = (
        attended.reshape(per_group, new_rows, HD)
        .transpose(1, 0, 2)
        .reshape(new_rows, per_group * HD)
    )
    fresh = jnp.concatenate([key_new, value_new], axis=1)
    appended = lax.dynamic_update_slice(cache_rows, fresh, (length, jnp.zeros((), jnp.int32)))
    return (attended, appended)


def local(
    tokens,
    attn_gain,
    qkv_weight,
    out_weight,
    mlp_gain,
    up_weight,
    down_weight,
    final_gain,
    head_weight,
    kv_cache,
    cache_lengths,
    slot_request,
):
    gx_count = lax.axis_size("gx")
    gy_count = lax.axis_size("gy")
    copies = gx_count // KVH
    gx_place = lax.axis_index("gx")
    copy_index = gx_place // KVH
    slot_index = lax.axis_index("gy") * copies + copy_index
    new_rows = tokens.shape[0] // copies
    feature_cols = tokens.shape[1]
    gathered_tokens = gather_features(tokens)
    tokens_f32 = gathered_tokens.astype(jnp.float32)
    normed = (tokens_f32 * rms_factor(tokens_f32) * attn_gain.astype(jnp.float32)).astype(
        jnp.bfloat16
    )
    projected = rows_product(normed, qkv_weight).astype(jnp.bfloat16)
    own_half = lax.dynamic_slice_in_dim(projected, copy_index * new_rows, new_rows, 0)
    sent_rows = lax.dynamic_slice_in_dim(projected, (1 - copy_index) * new_rows, new_rows, 0)
    received = pair_swap(sent_rows)
    group_cols = jnp.where(
        copy_index == 0,
        jnp.concatenate([own_half, received], axis=1),
        jnp.concatenate([received, own_half], axis=1),
    )
    length = cache_lengths[slot_request[slot_index]]
    attended, appended = attend_cache(group_cols, kv_cache[0], length, new_rows)
    new_cache = appended[None]
    half_width = attended.shape[1] // 2
    kept_half = lax.dynamic_slice_in_dim(attended, copy_index * half_width, half_width, 1)
    handed = lax.dynamic_slice_in_dim(attended, (1 - copy_index) * half_width, half_width, 1)
    returned = pair_swap(handed)
    attention_rows = jnp.where(
        copy_index == 0,
        jnp.concatenate([kept_half, returned], axis=0),
        jnp.concatenate([returned, kept_half], axis=0),
    )
    attention_terms = columns_product(attention_rows, out_weight)
    middle = (tokens.astype(jnp.float32) + scatter_partials(attention_terms)).astype(jnp.bfloat16)
    middle_full = gather_features(middle)
    middle_f32 = middle_full.astype(jnp.float32)
    mlp_input = (middle_f32 * rms_factor(middle_f32) * mlp_gain.astype(jnp.float32)).astype(
        jnp.bfloat16
    )
    up_values = rows_product(mlp_input, up_weight)
    rectified = jnp.maximum(up_values, 0.0)
    activation = (rectified * rectified).astype(jnp.bfloat16)
    down_terms = columns_product(activation, down_weight)
    hidden_out = (middle.astype(jnp.float32) + scatter_partials(down_terms)).astype(jnp.bfloat16)
    final_rows = hidden_out.reshape(copies, new_rows, feature_cols)[:, new_rows - 1, :]
    every_last = lax.all_gather(final_rows, ("gx", "gy"), axis=0, tiled=True)
    slot_rows = every_last.reshape(gx_count, gy_count, copies, feature_cols).transpose(1, 2, 0, 3)
    slot_rows = slot_rows.reshape(gy_count * copies, gx_count * feature_cols).astype(jnp.float32)
    mean_square = jnp.mean(slot_rows * slot_rows, axis=1)
    last_norms = jnp.sqrt(mean_square)
    head_input = (
        slot_rows * lax.rsqrt(mean_square + epsilon)[:, None] * final_gain.astype(jnp.float32)
    ).astype(jnp.bfloat16)
    logits = jnp.dot(head_input, head_weight, preferred_element_type=jnp.float32)
    max_logits = lax.pmax(jnp.max(logits, axis=1), ("gx", "gy"))
    return (hidden_out, new_cache, last_norms, max_logits, head_input)


def solution(mesh):
    in_specs = (
        P("gy", "gx"),
        P(),
        P("gy", "gx"),
        P("gx", "gy"),
        P(),
        P("gy", "gx"),
        P("gx", "gy"),
        P(),
        P(None, ("gx", "gy")),
        P(("gy", "gx"), None, None),
        P(),
        P(),
    )
    out_specs = (P("gy", "gx"), P(("gy", "gx"), None, None), P(), P(), P())
    return jax.shard_map(local, mesh=mesh, in_specs=in_specs, out_specs=out_specs, check_vma=False)
```

profile of v0, /device:TPU:1, one launch (start us, length us, event | category | flops | bytes accessed | tf_op | source)
XLA Modules:
  0.0 957.5 jit_solution(2756551729727596490)
XLA Ops:
  7.2 0.7 all-gather.8.cloned.1.call-update
  7.9 0.0 all-gather.10.cloned.1.call-start
  8.0 0.7 all-gather.10.cloned.1.call-update
  8.7 0.0 all-gather.12.cloned.1.call-start
  8.7 0.7 all-gather.12.cloned.1.call-update
  9.4 0.0 reduce-scatter.3.cloned.1.call-start
  9.5 0.6 dynamic_slice.21
  12.0 0.6 dynamic_slice.22
  13.4 81.3 %all-gather.8.cloned.1.call-done = bf16[256,4096]{1,0:T(8,128)(2,1)} async-done(((bf16[256,256]{1,0:T(8,128)(2,1)}), bf16[256,4096]{1,0:T(8,128)(2,1)}) %all-gather.8.cloned.1.call-update) | async-done | bytes 2097168 | tf_op jit(solution)/shard_map/all_gather | solution.py:32
  94.6 2.1 fusion.8
  96.7 39.1 %all-gather.10.cloned.1.call-done = bf16[4096,384]{1,0:T(8,128)(2,1)} async-done(((bf16[256,384]{1,0:T(8,128)(2,1)}), bf16[4096,384]{1,0:T(8,128)(2,1)}) %all-gather.10.cloned.1.call-update) | async-done | bytes 3145744 | tf_op jit(solution)/shard_map/all_gather | solution.py:38
  135.8 3.8 fusion.31
  139.7 5.5 collective-permute-start
  145.2 2.7 collective-permute-done
  147.9 0.1 maximum_select_fusion
  148.0 1.5 fusion.58
  149.6 4.9 while.14
  149.6 0.7 add_compare_fusion.2
  150.3 0.3 fusion.75
  150.6 0.2 fusion.76
  150.8 0.4 convolution_add_fusion.3
  151.2 0.7 add_compare_fusion.2
  151.9 0.3 fusion.75
  152.2 0.2 fusion.76
  152.5 0.4 convolution_add_fusion.3
  152.9 0.7 add_compare_fusion.2
  153.6 0.3 fusion.75
  153.9 0.2 fusion.76
  154.1 0.4 convolution_add_fusion.3
  154.5 0.7 max.14
  155.2 1.0 fusion.40
  156.2 1.2 fusion.36
  157.5 0.1 copy.23
  157.6 5.5 collective-permute-start.1
  163.2 14.0 %all-gather.12.cloned.1.call-done = bf16[256,4096]{1,0:T(8,128)(2,1)} async-done(((bf16[256,256]{1,0:T(8,128)(2,1)}), bf16[256,4096]{1,0:T(8,128)(2,1)}) %all-gather.12.cloned.1.call-update) | async-done | bytes 2097168 | tf_op jit(solution)/shard_map/all_gather | solution.py:46
  177.2 3.7 convolution_convert_fusion
  180.9 0.0 all-gather.14.cloned.1.call-start
  180.9 205.0 %reduce-scatter.3.cloned.1.call-done = bf16[256,256]{1,0:T(8,128)(2,1)} async-done(((bf16[256,4096]{1,0:T(8,128)(2,1)}), bf16[256,256]{1,0:T(8,128)(2,1)}) %reduce-scatter.3.cloned.1.call-update) | async-done | bytes 131088 | tf_op jit(solution)/shard_map/reduce_scatter | solution.py:56
  385.9 1.6 add_convert_fusion.1
  387.5 0.0 all-gather.16.cloned.1.call-start
  387.6 0.5 all-gather.16.cloned.1.call-update
  388.1 0.0 all-gather.18.cloned.1.call-start
  388.2 0.7 all-gather.18.cloned.1.call-update
  388.9 0.0 reduce-scatter.5.cloned.1.call-start
  388.9 83.5 %all-gather.14.cloned.1.call-done = bf16[256,4096]{1,0:T(8,128)(2,1)} async-done(((bf16[256,256]{1,0:T(8,128)(2,1)}), bf16[256,4096]{1,0:T(8,128)(2,1)}) %all-gather.14.cloned.1.call-update) | async-done | bytes 2097168 | tf_op jit(solution)/shard_map/all_gather | solution.py:32
  472.4 2.1 fusion.11
  474.5 45.9 %all-gather.16.cloned.1.call-done = bf16[4096,768]{1,0:T(8,128)(2,1)} async-done(((bf16[256,768]{1,0:T(8,128)(2,1)}), bf16[4096,768]{1,0:T(8,128)(2,1)}) %all-gather.16.cloned.1.call-update) | async-done | bytes 6291472 | tf_op jit(solution)/shard_map/all_gather | solution.py:38
  520.4 58.7 %all-gather.18.cloned.1.call-done = bf16[768,4096]{1,0:T(8,128)(2,1)} async-done(((bf16[768,256]{1,0:T(8,128)(2,1)}), bf16[768,4096]{1,0:T(8,128)(2,1)}) %all-gather.18.cloned.1.call-update) | async-done | bytes 6291472 | tf_op jit(solution)/shard_map/all_gather | solution.py:46
  579.1 11.1 %convolution_convert_fusion.1 = bf16[256,4096]{1,0:T(8,128)(2,1)} fusion(bf16[768,4096]{1,0:T(8,128)(2,1)} %all-gather.18.cloned.1.call-done, bf16[4096,768]{1,0:T(8,128)(2,1)} %all-gather.16.cloned.1.call-done, bf16[256,4096]{1,0:T(8,128)(2,1)} %all-gather.14.cloned.1.call-done, f32[4096]{0:T(1024)S(1)} %convert_element_type.90, f32[256]{0:T(256)S(1)} %add_rsqrt_fusion.1), kind=kOutput, calls=%fused_computation.18 | convolution fusion | flops 3227058176 | bytes 16794624 | tf_op jit(solution)/shard_map/dot_general | solution.py:44
  592.2 0.8 slice_bitcast_fusion
  593.0 201.4 %reduce-scatter.5.cloned.1.call-done = bf16[256,256]{1,0:T(8,128)(2,1)} async-done(((bf16[256,4096]{1,0:T(8,128)(2,1)}), bf16[256,256]{1,0:T(8,128)(2,1)}) %reduce-scatter.5.cloned.1.call-update) | async-done | bytes 131088 | tf_op jit(solution)/shard_map/reduce_scatter | solution.py:56
  794.5 0.9 add_convert_fusion
  795.4 72.9 %all-gather = bf16[512,1,256]{2,1,0:T(2,128)(2,1)S(1)} all-gather(bf16[2,1,256]{2,1,0:T(2,128)(2,1)S(1)} %slice.26), channel_id=2, replica_groups=mesh['gx'=16,'gy'=16] {'gx','gy'}, dimensions={0}, use_global_device_ids=true | all-gather | bytes 263168 | tf_op jit(solution)/shard_map/all_gather | solution.py:180
  868.4 2.2 convert_reduce_fusion
  870.6 0.3 reshape.92
  870.9 0.3 copy.24
  871.2 0.3 copy.26
  871.5 0.1 reduce_sum.56
  871.7 0.1 rsqrt.29
  871.8 0.1 multiply_convert_fusion
  871.9 3.2 convolution_reduce_fusion
  875.2 0.6 dynamic_update_slice.4
  875.8 74.3 %pmax.7 = f32[32]{0:T(128)} all-reduce(f32[32]{0:T(128)S(1)} %convolution_reduce_fusion), channel_id=1, replica_groups=mesh['gx'=16,'gy'=16] {'gx','gy'}, use_global_device_ids=true, to_apply=%region_13.14 | all-reduce | flops 32 | bytes 256 | tf_op jit(solution)/shard_map/pmax | solution.py:189
  950.1 0.6 sqrt.7
  (56 shorter events, 0.5 us)
Async XLA Ops:
  7.2 6.1 copy-start.7
  7.2 4.9 copy-start.11
  7.2 2.3 copy-start.10
  7.2 87.4 %all-gather.8.cloned.1.call-start = ((), (), s32[]{:S(2)}) async-start(), calls=%async_computation.2 | async-start | bytes 2228224 | tf_op jit(solution)/shard_map/all_gather | solution.py:32
  7.9 127.9 %all-gather.10.cloned.1.call-start = ((), (), s32[]{:S(2)}) async-start(), calls=%async_computation.3 | async-start | bytes 3342336 | tf_op jit(solution)/shard_map/all_gather | solution.py:38
  8.7 168.5 %all-gather.12.cloned.1.call-start = ((), (), s32[]{:S(2)}) async-start(), calls=%async_computation.4 | async-start | bytes 2228224 | tf_op jit(solution)/shard_map/all_gather | solution.py:46
  9.4 376.5 %reduce-scatter.3.cloned.1.call-start = ((), (), s32[]{:S(2)}) async-start(), calls=%async_computation.5 | async-start | bytes 2228224 | tf_op jit(solution)/shard_map/reduce_scatter | solution.py:56
  96.7 52.8 %copy-start.1 = (bf16[1,4096,256]{2,1,0:T(8,128)(2,1)S(1)}, bf16[1,4096,256]{2,1,0:T(8,128)(2,1)}, u32[]{:S(2)}) copy-start(bf16[1,4096,256]{2,1,0:T(8,128)(2,1)} %param.23) | copy-start | bytes 6291460
  139.7 8.2 collective-permute-start
  148.0 1.6 copy-start.4
  157.6 19.5 %collective-permute-start.1 = (bf16[128,256]{0,1:T(8,128)(2,1)S(1)}, bf16[128,256]{0,1:T(8,128)(2,1)S(1)}, u32[]{:S(2)}, u32[]{:S(2)}) collective-permute-start(bf16[128,256]{0,1:T(8,128)(2,1)S(1)} %get-tuple-element.80), channel_id=1, source_target_pairs={{0,128},{128,0},{16,144},{144,16},{32,160},{160,32},{48,176},{176,... | collective-permute-start | bytes 196616 | tf_op jit(solution)/shard_map/ppermute | solution.py:24
  177.1 208.8 %copy-start.5 = (bf16[256,256]{1,0:T(8,128)(2,1)S(1)}, bf16[256,256]{1,0:T(8,128)(2,1)}, u32[]{:S(2)}) copy-start(bf16[256,256]{1,0:T(8,128)(2,1)} %param.14) | copy-start | bytes 393220
  177.1 211.8 %copy-start.8 = (bf16[4096]{0:T(1024)(128)(2,1)S(1)}, bf16[4096]{0:T(1024)(128)(2,1)}, u32[]{:S(2)}) copy-start(bf16[4096]{0:T(1024)(128)(2,1)} %param.18) | copy-start | bytes 24580
  180.9 291.6 %all-gather.14.cloned.1.call-start = ((), (), s32[]{:S(2)}) async-start(), calls=%async_computation.6 | async-start | bytes 2228224 | tf_op jit(solution)/shard_map/all_gather | solution.py:32
  387.5 132.8 %all-gather.16.cloned.1.call-start = ((), (), s32[]{:S(2)}) async-start(), calls=%async_computation.7 | async-start | bytes 6684672 | tf_op jit(solution)/shard_map/all_gather | solution.py:38
  388.1 190.9 %all-gather.18.cloned.1.call-start = ((), (), s32[]{:S(2)}) async-start(), calls=%async_computation.8 | async-start | bytes 6684672 | tf_op jit(solution)/shard_map/all_gather | solution.py:46
  388.9 405.6 %reduce-scatter.5.cloned.1.call-start = ((), (), s32[]{:S(2)}) async-start(), calls=%async_computation.9 | async-start | bytes 2228224 | tf_op jit(solution)/shard_map/reduce_scatter | solution.py:56
  474.5 117.0 %copy-start.9 = (bf16[4096]{0:T(1024)(128)(2,1)S(1)}, bf16[4096]{0:T(1024)(128)(2,1)}, u32[]{:S(2)}) copy-start(bf16[4096]{0:T(1024)(128)(2,1)} %param.21) | copy-start | bytes 24580
  474.5 320.0 %copy-start.2 = (bf16[256,256]{1,0:T(8,128)(2,1)S(1)}, bf16[256,256]{1,0:T(8,128)(2,1)}, u32[]{:S(2)}) copy-start(bf16[256,256]{1,0:T(8,128)(2,1)} %add_convert_fusion.1) | copy-start | bytes 393220
  795.4 79.8 %copy-start.6 = (bf16[256,256]{1,0:T(8,128)(2,1)}, bf16[256,256]{1,0:T(8,128)(2,1)S(1)}, u32[]{:S(2)}) copy-start(bf16[256,256]{1,0:T(8,128)(2,1)S(1)} %add_convert_fusion) | copy-start | bytes 393220
  871.9 78.7 %copy-start.3 = (bf16[32,4096]{1,0:T(8,128)(2,1)}, bf16[32,4096]{1,0:T(8,128)(2,1)S(1)}, u32[]{:S(2)}) copy-start(bf16[32,4096]{1,0:T(8,128)(2,1)S(1)} %multiply_convert_fusion) | copy-start | bytes 786436
  875.8 74.9 %copy-start = (bf16[1,4096,256]{2,1,0:T(8,128)(2,1)}, bf16[1,4096,256]{2,1,0:T(8,128)(2,1)S(1)}, u32[]{:S(2)}) copy-start(bf16[1,4096,256]{2,1,0:T(8,128)(2,1)S(1)} %dynamic_update_slice.4) | copy-start | bytes 6291460
Sparse Core Ops, SparseCore 0:
  10.5 84.1 all-gather.7
  96.5 39.2 all-gather.9
  137.6 39.5 all-gather.11
  181.5 204.4 reduce-scatter.2
  388.8 83.5 all-gather.13
  474.1 46.2 all-gather.15
  522.1 56.8 all-gather.17
  590.3 204.0 reduce-scatter.4
where the time goes:
time: 958 us
  waiting for transfers between devices  735 us (77%)
  blocking collectives  147 us (15%)
  matrix products  26.7 us (3%)
  between operations  19.1 us (2%)
  other arithmetic  13.5 us (1%)
  starting transfers between devices  11.4 us (1%)
    reduce_scatter x2, waiting for transfers between devices, scatter_partials(): lax.psum_scatter(partial_terms.astype(jnp.bfloat16), 'gx', scatter_dimens...  406 us
    all_gather x2, waiting for transfers between devices, gather_features(): return lax.all_gather(shard_rows, 'gx', axis=1, tiled=True)  165 us
    all_gather x2, waiting for transfers between devices, rows_product(): lax.all_gather(weight_shard, 'gy', axis=0, tiled=True)  84.9 us
    pmax x1, blocking collectives, local(): max_logits = lax.pmax(jnp.max(logits, axis=1), ('gx', 'gy'))  74.3 us
    all_gather x1, blocking collectives, local(): every_last = lax.all_gather(final_rows, ('gx', 'gy'), axis=0, tiled=True)  72.9 us
    all_gather x2, waiting for transfers between devices, columns_product(): lax.all_gather(weight_shard, 'gy', axis=1, tiled=True)  72.7 us
  transfers between devices with their start and end apart: 10, of which 9 were waited for; matrix products, arithmetic and copies ran while one was open for 2% of the time, Pallas kernels for 0%

commit v1 on v0

v1 whole, which is shorter than its diff:
```python
import math

import jax
import jax.numpy as jnp
from jax import lax
from jax.experimental import pallas as pl
from jax.experimental.pallas import tpu as pltpu
from jax.sharding import PartitionSpec as P

HEADS = 32
KVH = 8
HD = 128
PER = HEADS // KVH
BF = jnp.bfloat16
F32 = jnp.float32

epsilon = 1e-05
negative = -1e30

GX = 16
GY = 16
NZ = 8
RIGHT_LIMIT = (4, 3)
LEFT_LIMIT = (3, 4)


class Copies:
    def __init__(self, send_sems, recv_sems):
        self.send_sems, self.recv_sems = send_sems, recv_sems
        self.names, self.sent = {}, []

    def index(self, name):
        return self.names.setdefault(name, len(self.names))

    def make(self, name, source, target, peer):
        at = self.index(name)
        return pltpu.make_async_remote_copy(
            src_ref=source,
            dst_ref=target,
            send_sem=self.send_sems.at[at],
            recv_sem=self.recv_sems.at[at],
            device_id=peer,
            device_id_type=pl.DeviceIdType.MESH,
        )

    def send(self, name, source, target, peer):
        copy = self.make(name, source, target, peer)
        copy.start()
        self.sent.append(copy)

    def arrive(self, name, target, peer):
        self.make(name, target, target, peer).wait_recv()

    def drain(self):
        for copy in self.sent:
            copy.wait_send()
        self.sent = []


def gx_at(dz, flip):
    place = lax.axis_index("gx")
    z, x = place // 2, place % 2
    return lax.rem(z + dz + NZ, NZ) * 2 + (1 - x if flip else x)


def gy_at(dx, dy, dc):
    place = lax.axis_index("gy")
    x, y, c = place // 8, (place // 2) % 4, place % 2
    return lax.rem(x + dx, 2) * 8 + lax.rem(y + dy + 4, 4) * 2 + lax.rem(c + dc, 2)


def gx_peer(dz, flip):
    return {"gx": gx_at(dz, flip)}


def gy_peer(dx, dy, dc):
    return {"gy": gy_at(dx, dy, dc)}


def greet(peers):
    barrier = pltpu.get_barrier_semaphore()
    for peer in peers:
        pl.semaphore_signal(barrier, inc=1, device_id=peer, device_id_type=pl.DeviceIdType.MESH)
    pl.semaphore_wait(barrier, len(peers))


GX_NEAR = ((1, 0), (-1, 0), (0, 1))
GY_NEAR = ((1, 0, 0), (0, 1, 0), (0, -1, 0), (0, 0, 1))


def gather_gx(copies, tag, own, slot, pieces, arrived):
    span = range(pieces)

    def push(way, flip, far, piece, source, origin):
        step = 1 if way == "R" else -1
        copies.send((tag, way, flip, far, piece), source, slot(origin, piece), gx_peer(step, 0))

    me = gx_at(0, 0)
    partner = gx_at(0, 1)
    for piece in span:
        push("R", 0, 1, piece, own(piece), me)
        push("L", 0, 1, piece, own(piece), me)
        copies.send((tag, "X", piece), own(piece), slot(me, piece), gx_peer(0, 1))
    yield

    def take(way, flip, far):
        limit = (RIGHT_LIMIT if way == "R" else LEFT_LIMIT)[flip]
        if far > limit:
            return
        origin = gx_at(-far if way == "R" else far, flip)
        for piece in span:
            here = slot(origin, piece)
            copies.arrive((tag, way, flip, far, piece), here, gx_peer(0, 1))
            if far < limit:
                push(way, flip, far + 1, piece, here, origin)
        for piece in span:
            arrived(origin, piece)

    for far in range(1, 6):
        take("R", 0, far)
        take("L", 0, far)
        yield
        if far == 1:
            for piece in span:
                here = slot(partner, piece)
                copies.arrive((tag, "X", piece), here, gx_peer(0, 1))
                push("R", 1, 1, piece, here, partner)
                push("L", 1, 1, piece, here, partner)
            for piece in span:
                arrived(partner, piece)
        else:
            take("R", 1, far - 1)
            take("L", 1, far - 1)
        yield


def gather_gy(copies, tag, own, slot):
    def push(name, source, origin, *step):
        copies.send((tag,) + name, source, slot(origin), gy_peer(*step))

    def share(dx, dy):
        origin = gy_at(dx, dy, 0)
        source = own if (dx, dy) == (0, 0) else slot(origin)
        push(("S", dx, dy % 4), source, origin, 0, 0, 1)

    def take(name, dx, dy):
        origin = gy_at(dx, dy, 0)
        here = slot(origin)
        copies.arrive((tag,) + name, here, gy_peer(0, 0, 1))
        return here, origin

    me = gy_at(0, 0, 0)
    push(("X",), own, me, 1, 0, 0)
    push(("U", 0, 1), own, me, 0, 1, 0)
    push(("D", 0, 1), own, me, 0, -1, 0)
    share(0, 0)
    yield
    here, origin = take(("X",), 1, 0)
    push(("U", 1, 1), here, origin, 0, 1, 0)
    push(("D", 1, 1), here, origin, 0, -1, 0)
    share(1, 0)
    yield
    here, origin = take(("U", 0, 1), 0, -1)
    push(("U", 0, 2), here, origin, 0, 1, 0)
    share(0, -1)
    take(("D", 0, 1), 0, 1)
    share(0, 1)
    yield
    here, origin = take(("D", 1, 1), 1, 1)
    push(("D", 1, 2), here, origin, 0, -1, 0)
    share(1, 1)
    take(("U", 1, 1), 1, -1)
    share(1, -1)
    yield
    take(("U", 0, 2), 0, -2)
    share(0, -2)
    take(("D", 1, 2), 1, 2)
    share(1, 2)
    yield
    for dx in (0, 1):
        for dy in range(4):
            copies.arrive((tag, "S", dx, dy), slot(gy_at(dx, dy, 1)), gy_peer(0, 0, 1))
    yield


def advance(*flows):
    for flow in flows:
        next(flow, None)


def finish(*flows):
    for flow in flows:
        for _ in flow:
            pass


def rows_at(index, count):
    return pl.ds(pl.multiple_of(index * count, count), count)


def square_sum(block):
    values = block.astype(F32)
    return jnp.sum(values * values, axis=1, keepdims=True)


def normalize(blocks, squares, gain, normed, width):
    factor = lax.rsqrt(squares[...] * (1.0 / (GX * width)) + epsilon)

    def one(at, _):
        columns = rows_at(at, width)
        values = blocks[at].astype(F32) * factor * gain[:, columns].astype(F32)
        normed[:, columns] = values.astype(BF)
        return _

    lax.fori_loop(0, GX, one, 0)


def project_kernel(
    tokens, gain, weight, out_shard, group, out_full,
    blocks, weights, out_mine, squares, normed, outgoing, incoming, send_sems, recv_sems, local_sem,
):
    rows, width = tokens.shape
    half = rows // 2
    depth = weight.shape[0]
    copies = Copies(send_sems, recv_sems)
    gx, gy = lax.axis_index("gx"), lax.axis_index("gy")
    turned = {"gx": gy, "gy": gx}
    diagonal = gx == gy
    greet(
        [gx_peer(*step) for step in GX_NEAR + ((4, 0),)]
        + [gy_peer(*step) for step in GY_NEAR]
        + [turned]
    )

    def slot(origin, piece):
        return blocks.at[origin]

    def arrived(origin, piece):
        squares[...] += square_sum(blocks[origin])

    feed = gather_gx(copies, "t", lambda piece: tokens, slot, 1, arrived)
    advance(feed)
    load = gather_gy(copies, "w", weight, lambda origin: weights.at[rows_at(origin, depth), :])
    advance(load)
    turn = copies.make(("turn",), out_shard, out_mine, turned)

    @pl.when(gx != gy)
    def _():
        turn.start()

    blocks[gx] = tokens[...]
    weights[rows_at(gy, depth), :] = weight[...]
    squares[...] = square_sum(tokens[...])

    @pl.when(diagonal)
    def _():
        out_mine[...] = out_shard[...]

    advance(feed)
    advance(feed)

    @pl.when(gx != gy)
    def _():
        turn.wait()

    def out_slot(origin):
        return out_full.at[rows_at(origin, depth), :]

    keep = pltpu.make_async_copy(out_mine, out_slot(gy), local_sem)
    keep.start()
    out_load = gather_gy(copies, "o", out_mine, out_slot)
    advance(load)
    advance(feed)
    advance(load)
    advance(feed)
    advance(load, out_load)
    for _ in feed:
        advance(load, out_load)
    finish(load)
    advance(out_load)

    normalize(blocks, squares, gain, normed, width)
    mine = gx // KVH
    outgoing[...] = jnp.dot(
        normed[rows_at(1 - mine, half), :], weights[...], preferred_element_type=F32
    ).astype(BF)
    copies.send(("swap",), outgoing, incoming, gx_peer(4, 0))
    group[mine] = jnp.dot(
        normed[rows_at(mine, half), :], weights[...], preferred_element_type=F32
    ).astype(BF)
    finish(out_load)
    copies.arrive(("swap",), incoming, gx_peer(4, 0))
    group[1 - mine] = incoming[...]
    keep.wait()
    copies.drain()


def attend_kernel(lengths, requests, group, cache, attended, new_cache, held, shifted, load_sem, store_sem, patch_sem):
    capacity = cache.shape[1]
    new = group.shape[1]
    queries = PER * new
    block = 512
    load = pltpu.make_async_copy(cache.at[0], held, load_sem)
    load.start()
    gx, gy = lax.axis_index("gx"), lax.axis_index("gy")
    slot = gy * 2 + gx // KVH
    length = lengths[requests[slot]]
    scaling = 1.0 / math.sqrt(HD)
    query = jnp.concatenate(
        [group[0, :, 0:HD], group[0, :, HD : 2 * HD], group[0, :, 2 * HD :], group[1, :, 0:HD]], axis=0
    )
    fresh = group[1, :, HD:]
    window = shifted.shape[0]
    base = pl.multiple_of(jnp.minimum(length // 16 * 16, capacity - window), 16)
    offset = length - base
    at = lax.broadcasted_iota(jnp.int32, (window, new), 0)
    token = lax.broadcasted_iota(jnp.int32, (window, new), 1)
    pick = jnp.where(at == token + offset, 1.0, 0.0).astype(BF)
    moved = jnp.dot(pick, fresh, preferred_element_type=F32)
    row = lax.broadcasted_iota(jnp.int32, (window, 2 * HD), 0)
    inside = jnp.logical_and(row >= offset, row < offset + new)
    load.wait()
    shifted[...] = jnp.where(inside, moved, held[pl.ds(base, window), :].astype(F32)).astype(BF)
    held[pl.ds(base, window), :] = shifted[...]
    store = pltpu.make_async_copy(held, new_cache.at[0], store_sem)
    store.start()

    key_at = lax.broadcasted_iota(jnp.int32, (block, queries), 0)
    ahead = key_at - lax.rem(lax.broadcasted_iota(jnp.int32, (block, queries), 1), new)

    def visit(step, carried):
        top, total, numerator = carried
        keys = rows_at(step, block)
        scores = lax.dot_general(
            held[keys, 0:HD], query, (((1,), (1,)), ((), ())), preferred_element_type=F32
        ) * scaling
        scores = jnp.where(ahead + step * block <= length, scores, negative)
        new_top = jnp.maximum(top, jnp.max(scores, axis=0, keepdims=True))
        factor = jnp.exp(top - new_top)
        weights = jnp.exp(scores - new_top)
        total = total * factor + jnp.sum(weights, axis=0, keepdims=True)
        numerator = numerator * factor + lax.dot_general(
            held[keys, HD:], weights.astype(BF), (((0,), (0,)), ((), ())), preferred_element_type=F32
        )
        return new_top, total, numerator

    initial = (
        jnp.full((1, queries), negative, F32),
        jnp.zeros((1, queries), F32),
        jnp.zeros((HD, queries), F32),
    )
    steps = (length + new + block - 1) // block
    top, total, numerator = lax.fori_loop(0, steps, visit, initial)
    result = numerator / total
    for head in range(PER):
        columns = slice(head % 2 * HD, head % 2 * HD + HD)
        attended[head // 2, :, columns] = result[:, head * new : (head + 1) * new].T.astype(BF)
    store.wait()


def feed_kernel(
    tokens, attended, out_full, gain, up_shard, down_shard, hidden, last,
    gathered, out_w, up_w, down_w, middle, blocks, squares, normed, active, stage, landing, crossing,
    partial, total, own_last, lasts, send_sems, recv_sems, local_sems,
):
    rows, width = tokens.shape
    half = rows // 2
    copies = Copies(send_sems, recv_sems)
    gx, gy = lax.axis_index("gx"), lax.axis_index("gy")
    greet([gx_peer(*step) for step in GX_NEAR] + [gy_peer(*step) for step in GY_NEAR])

    def att_slot(origin, piece):
        return gathered.at[piece * KVH + lax.rem(origin, KVH), rows_at(origin // KVH, half), :]

    flow = gather_gx(copies, "a", lambda piece: attended.at[piece], att_slot, 2, lambda origin, piece: None)
    advance(flow)
    depth = up_shard.shape[0]
    up_load = gather_gy(copies, "u", up_shard, lambda origin: up_w.at[rows_at(origin, depth), :])
    down_load = gather_gy(copies, "d", down_shard, lambda origin: down_w.at[origin])
    advance(up_load)
    fetch = pltpu.make_async_copy(out_full, out_w, local_sems.at[0])
    fetch.start()
    keep_up = pltpu.make_async_copy(up_shard, up_w.at[rows_at(gy, depth), :], local_sems.at[1])
    keep_up.start()
    keep_down = pltpu.make_async_copy(down_shard, down_w.at[gy], local_sems.at[2])
    keep_down.start()
    for piece in range(2):
        gathered[piece * KVH + lax.rem(gx, KVH), rows_at(gx // KVH, half), :] = attended[piece]
    for count, _ in enumerate(flow):
        if count == 4:
            advance(up_load, down_load)
        if count == 6:
            advance(up_load)
        if count == 8:
            advance(up_load, down_load)
    fetch.wait()
    sums = tokens[...].astype(F32)
    acc = jnp.zeros((rows, width), F32)
    for at in range(GX):
        acc = acc + jnp.dot(
            gathered[at], out_w[at * width : (at + 1) * width, :], preferred_element_type=F32
        )
    middle[...] = (sums + acc).astype(BF)

    def mid_slot(origin, piece):
        return blocks.at[origin, piece * half : (piece + 1) * half, :]

    def arrived(origin, piece):
        part = slice(piece * half, (piece + 1) * half)
        squares[part, :] += square_sum(blocks[origin, part, :])

    flow = gather_gx(copies, "m", lambda piece: middle.at[piece * half : (piece + 1) * half, :], mid_slot, 2, arrived)
    advance(flow)
    blocks[gx] = middle[...]
    squares[...] = square_sum(middle[...])
    for count, _ in enumerate(flow):
        if count == 1:
            advance(up_load, down_load)
        if count == 4:
            advance(up_load, down_load)
        if count == 6:
            advance(down_load)
    finish(up_load)
    normalize(blocks, squares, gain, normed, width)
    keep_up.wait()

    def unit(at, _):
        columns = rows_at(at, width)
        values = jnp.dot(normed[...], up_w[:, columns], preferred_element_type=F32)
        values = jnp.maximum(values, 0.0)
        active[:, columns] = (values * values).astype(BF)
        return _

    lax.fori_loop(0, active.shape[1] // width, unit, 0)
    keep_down.wait()
    finish(down_load)

    def share(origin):
        return jnp.dot(active[...], down_w[origin], preferred_element_type=F32)

    chains = (("L", 1, 4), ("R", 1, 3), ("R", 0, 4), ("L", 0, 3))
    spots = {}
    for way, flip, limit in chains:
        for left in range(limit):
            spots[way, flip, left] = len(spots)

    def toward(way, flip, left):
        return gx_at(left if way == "R" else -left, flip)

    def pass_on(way, flip, left, source):
        copies.send(
            ("r", way, flip, left),
            source,
            landing.at[spots[way, flip, left - 1]],
            gx_peer(1 if way == "R" else -1, 0),
        )

    for at, (way, flip, limit) in enumerate(chains):
        stage[at] = share(toward(way, flip, limit)).astype(BF)
        pass_on(way, flip, limit, stage.at[at])
    total[1] = share(gx_at(0, 1))
    total[0] = share(gx) + middle[...].astype(F32)
    for turn in range(1, 5):
        for way, flip, limit in chains:
            left = limit - turn
            if left < 0:
                continue
            spot = spots[way, flip, left]
            if left > 0:
                partial[...] = share(toward(way, flip, left))
            copies.arrive(("r", way, flip, left + 1), landing.at[spot], gx_peer(0, 1))
            if left > 0:
                landing[spot] = (landing[spot].astype(F32) + partial[...]).astype(BF)
                pass_on(way, flip, left, landing.at[spot])
            else:
                total[flip] += landing[spot].astype(F32)
                if (way, flip) == ("L", 1):
                    crossing[0] = total[1].astype(BF)
                    copies.send(("r", "X"), crossing.at[0], crossing.at[1], gx_peer(0, 1))
    copies.arrive(("r", "X"), crossing.at[1], gx_peer(0, 1))
    result = (total[0] + crossing[1].astype(F32)).astype(BF)
    hidden[...] = result
    total[0] = result.astype(F32)
    lane = width // 2
    for slot in range(2):
        for side in range(2):
            last[2 * slot + side : 2 * slot + side + 1, :] = total[
                0, slot * half + half - 1 : slot * half + half, side * lane : (side + 1) * lane
            ]
    copies.drain()


def spread_kernel(own, result, row, send_sems, recv_sems):
    copies = Copies(send_sems, recv_sems)
    gx, gy = lax.axis_index("gx"), lax.axis_index("gy")
    xs = [lax.rem(gx + step, GX) for step in range(1, GX)]
    ys = [lax.rem(gy + step, GY) for step in range(1, GY)]
    greet([{"gx": at} for at in xs] + [{"gy": at} for at in ys])
    for step, at in enumerate(xs):
        copies.send(("x", step), own, row.at[gx], {"gx": at})
    row[gx] = own[...]
    for step in range(GX - 1):
        copies.arrive(("x", step), row.at[lax.rem(gx + GX - 1 - step, GX)], {"gx": xs[0]})
    for step, at in enumerate(ys):
        copies.send(("y", step), row, result.at[gy], {"gy": at})
    result[gy] = row[...]
    for step in range(GY - 1):
        copies.arrive(("y", step), result.at[lax.rem(gy + GY - 1 - step, GY)], {"gy": ys[0]})
    copies.drain()


def largest_kernel(own, result, row, column, best, send_sems, recv_sems):
    copies = Copies(send_sems, recv_sems)
    gx, gy = lax.axis_index("gx"), lax.axis_index("gy")
    xs = [lax.rem(gx + step, GX) for step in range(1, GX)]
    ys = [lax.rem(gy + step, GY) for step in range(1, GY)]
    greet([{"gx": at} for at in xs] + [{"gy": at} for at in ys])
    for step, at in enumerate(ys):
        copies.send(("y", step), own, column.at[gy], {"gy": at})
    column[gy] = own[...]
    for step in range(GY - 1):
        copies.arrive(("y", step), column.at[lax.rem(gy + GY - 1 - step, GY)], {"gy": ys[0]})
    best[...] = jnp.max(column[...], axis=0)
    for step, at in enumerate(xs):
        copies.send(("x", step), best, row.at[gx], {"gx": at})
    row[gx] = best[...]
    for step in range(GX - 1):
        copies.arrive(("x", step), row.at[lax.rem(gx + GX - 1 - step, GX)], {"gx": xs[0]})
    result[...] = jnp.max(row[...], axis=0)
    copies.drain()


VM = pl.BlockSpec(memory_space=pltpu.VMEM)
SM = pl.BlockSpec(memory_space=pltpu.SMEM)
ANY = pl.BlockSpec(memory_space=pl.ANY)


def sems(count):
    return [pltpu.SemaphoreType.DMA((count,)), pltpu.SemaphoreType.DMA((count,))]


def params(collective):
    return pltpu.CompilerParams(collective_id=collective, has_side_effects=True)


def local(
    tokens,
    attn_gain,
    qkv_weight,
    out_weight,
    mlp_gain,
    up_weight,
    down_weight,
    final_gain,
    head_weight,
    kv_cache,
    cache_lengths,
    slot_request,
):
    rows, width = tokens.shape
    half = rows // 2
    model = GX * width
    columns = qkv_weight.shape[1]
    units = up_weight.shape[1]
    shape = jax.ShapeDtypeStruct
    group, out_full = pl.pallas_call(
        project_kernel,
        name="project",
        out_shape=[shape((2, half, columns), BF), shape((model, width), BF)],
        in_specs=[VM] * 4,
        out_specs=[VM, ANY],
        scratch_shapes=[
            pltpu.VMEM((GX, rows, width), BF),
            pltpu.VMEM((model, columns), BF),
            pltpu.VMEM((width, width), BF),
            pltpu.VMEM((rows, 1), F32),
            pltpu.VMEM((rows, model), BF),
            pltpu.VMEM((half, columns), BF),
            pltpu.VMEM((half, columns), BF),
        ]
        + sems(50)
        + [pltpu.SemaphoreType.DMA(())],
        compiler_params=params(0),
    )(tokens, attn_gain[None], qkv_weight, out_weight)
    window = half + 16
    attended, new_cache = pl.pallas_call(
        attend_kernel,
        name="attend",
        out_shape=[shape((2, half, 2 * HD), BF), shape(kv_cache.shape, BF)],
        in_specs=[SM, SM, VM, ANY],
        out_specs=[VM, ANY],
        scratch_shapes=[
            pltpu.VMEM(kv_cache.shape[1:], BF),
            pltpu.VMEM((window, 2 * HD), BF),
            pltpu.SemaphoreType.DMA(()),
            pltpu.SemaphoreType.DMA(()),
            pltpu.SemaphoreType.DMA(()),
        ],
    )(cache_lengths, slot_request, group, kv_cache)
    hidden_out, last = pl.pallas_call(
        feed_kernel,
        name="feed",
        out_shape=[shape((rows, width), BF), shape((4, width // 2), F32)],
        in_specs=[VM, VM, ANY, VM, VM, VM],
        out_specs=[VM, VM],
        scratch_shapes=[
            pltpu.VMEM((GX, rows, width), BF),
            pltpu.VMEM((model, width), BF),
            pltpu.VMEM((model, units), BF),
            pltpu.VMEM((GX, units, width), BF),
            pltpu.VMEM((rows, width), BF),
            pltpu.VMEM((GX, rows, width), BF),
            pltpu.VMEM((rows, 1), F32),
            pltpu.VMEM((rows, model), BF),
            pltpu.VMEM((rows, units), BF),
            pltpu.VMEM((4, rows, width), BF),
            pltpu.VMEM((14, rows, width), BF),
            pltpu.VMEM((2, rows, width), BF),
            pltpu.VMEM((rows, width), F32),
            pltpu.VMEM((2, rows, width), F32),
            pltpu.VMEM((4, width // 2), F32),
            pltpu.VMEM((8, width // 2), F32),
        ]
        + sems(110)
        + [pltpu.SemaphoreType.DMA((3,))],
        compiler_params=params(1),
    )(tokens, attended, out_full, mlp_gain[None], up_weight, down_weight)
    every_last = pl.pallas_call(
        spread_kernel,
        name="spread",
        out_shape=shape((GY, GX, 4, width // 2), F32),
        in_specs=[VM],
        out_specs=VM,
        scratch_shapes=[pltpu.VMEM((GX, 4, width // 2), F32)] + sems(30),
        compiler_params=params(2),
    )(last)
    slot_rows = every_last.reshape(GY, GX, 2, width).transpose(0, 2, 1, 3).reshape(2 * GY, model)
    mean_square = jnp.mean(slot_rows * slot_rows, axis=1)
    last_norms = jnp.sqrt(mean_square)
    head_input = (
        slot_rows * lax.rsqrt(mean_square + epsilon)[:, None] * final_gain.astype(F32)
    ).astype(BF)
    logits = jnp.dot(head_input, head_weight, preferred_element_type=F32)
    own_best = jnp.pad(jnp.max(logits, axis=1), (0, 128 - 2 * GY))[None]
    best = pl.pallas_call(
        largest_kernel,
        name="largest",
        out_shape=shape((1, 128), F32),
        in_specs=[VM],
        out_specs=VM,
        scratch_shapes=[
            pltpu.VMEM((GX, 1, 128), F32),
            pltpu.VMEM((GY, 1, 128), F32),
            pltpu.VMEM((1, 128), F32),
        ]
        + sems(30),
        compiler_params=params(3),
    )(own_best)
    max_logits = best[0, : 2 * GY]
    return (hidden_out, new_cache, last_norms, max_logits, head_input)


def solution(mesh):
    in_specs = (
        P("gy", "gx"),
        P(),
        P("gy", "gx"),
        P("gx", "gy"),
        P(),
        P("gy", "gx"),
        P("gx", "gy"),
        P(),
        P(None, ("gx", "gy")),
        P(("gy", "gx"), None, None),
        P(),
        P(),
    )
    out_specs = (P("gy", "gx"), P(("gy", "gx"), None, None), P(), P(), P())
    return jax.shard_map(local, mesh=mesh, in_specs=in_specs, out_specs=out_specs, check_vma=False)
```

time: 958 us -> 220 us (0.23)
  waiting for transfers between devices: 735 us -> 0 us
  Pallas kernels: 0 us -> 208 us
  blocking collectives: 147 us -> 0 us
  matrix products: 26.7 us -> 3.21 us
  between operations: 19.1 us -> 0.74 us
  other arithmetic: 13.5 us -> 0.43 us
  starting transfers between devices: 11.4 us -> 0 us
    reduce_scatter x2 -> x0, waiting for transfers between devices: 406 us -> none  [scatter_partials(): lax.psum_scatter(partial_terms.astype(jnp.bfloat16), 'gx', scatter_dimens...]
    all_gather x6 -> x0, waiting for transfers between devices: 322 us -> none  [the longest x2 165 us: gather_features(): return lax.all_gather(shard_rows, 'gx', axis=1, tiled=True)]
    pallas_call x0 -> x5, Pallas kernels: none -> 208 us  [the longest x1 101 us: local(): pl.pallas_call(feed_kernel, name='feed', out_shape=[shape((rows, width),...]
    pmax x1 -> x0, blocking collectives: 74.3 us -> none  [local(): max_logits = lax.pmax(jnp.max(logits, axis=1), ('gx', 'gy'))]
    all_gather x1 -> x0, blocking collectives: 72.9 us -> none  [local(): every_last = lax.all_gather(final_rows, ('gx', 'gy'), axis=0, tiled=True)]
    dot_general x12 -> x1, matrix products: 26.7 us -> 3.21 us  [local(): logits = jnp.dot(head_input, head_weight, preferred_element_type=F32)]
    ppermute x2 -> x0, starting transfers between devices: 11.1 us -> none  [from_partner(): return lax.ppermute(block, axis, route)]
  transfers between devices with their start and end apart: 10 -> 0, of which waited for: 9 -> 0; matrix products, arithmetic and copies ran while one was open for 2% -> 0% of each run, Pallas kernels for 0% -> 0%
where the time goes in v1:
time: 220 us
  Pallas kernels  208 us (95%)
  local copies, waits for them, and re-layouts  7.51 us (3%)
  matrix products  3.21 us (1%)
    pallas_call x1, Pallas kernels, local(): pl.pallas_call(feed_kernel, name='feed', out_shape=[shape((rows, width),...  101 us
    pallas_call x1, Pallas kernels, local(): pl.pallas_call(project_kernel, name='project', out_shape=[shape((2, half,...  65.3 us
    pallas_call x1, Pallas kernels, local(): pl.pallas_call(spread_kernel, name='spread', out_shape=shape((GY, GX, 4,...  19.9 us
    pallas_call x1, Pallas kernels, local(): pl.pallas_call(largest_kernel, name='largest', out_shape=shape((1, 128),...  16.7 us
    pallas_call x1, Pallas kernels, local(): pl.pallas_call(attend_kernel, name='attend', out_shape=[shape((2, half, 2...  5.15 us

profile of v1, /device:TPU:1, one launch (start us, length us, event | category | flops | bytes accessed | tf_op | source)
XLA Modules:
  0.0 220.0 jit_solution(5390345324821101379)
XLA Ops:
  0.6 1.3 broadcast_in_dim.11.gain
  1.9 65.3 %project.1 = (bf16[2,128,384]{2,1,0:T(8,128)(2,1)}, bf16[4096,256]{1,0:T(8,128)(2,1)}) custom-call(bf16[256,256]{1,0:T(8,128)(2,1)} %tokens.3, bf16[1,4096]{1,0:T(2,128)(2,1)} %broadcast_in_dim.11.gain, bf16[256,384]{1,0:T(8,128)(2,1)} %weight.1, bf16[256,256]{1,0:T(8,128)(2,1)} %out_shard.1), custom_call_target="tpu_custom_call" | custom-call | tf_op jit(solution)/shard_map/project/pallas_call | solution.py:566
  67.3 5.1 %attend.1 = (bf16[2,128,256]{2,1,0:T(8,128)(2,1)}, bf16[1,4096,256]{2,1,0:T(8,128)(2,1)}) custom-call(s32[32]{0:T(128)} %lengths.1, s32[32]{0:T(128)} %requests.1, bf16[2,128,384]{2,1,0:T(8,128)(2,1)} %get-tuple-element.11.group, bf16[1,4096,256]{2,1,0:T(8,128)(2,1)} %cache.1), custom_call_target="tpu_custom_call" | custom-call | tf_op jit(solution)/shard_map/attend/pallas_call | solution.py:586
  72.4 0.0 copy-start.2
  72.5 1.3 broadcast_in_dim.12.gain
  73.8 101.1 %feed.1 = (bf16[256,256]{1,0:T(8,128)(2,1)}, f32[4,128]{1,0:T(4,128)}) custom-call(bf16[256,256]{1,0:T(8,128)(2,1)} %tokens.3, bf16[2,128,256]{2,1,0:T(8,128)(2,1)} %get-tuple-element.12.attended, bf16[4096,256]{1,0:T(8,128)(2,1)} %get-tuple-element.13.out_full, bf16[1,4096]{1,0:T(2,128)(2,1)} %broadcast_in_dim.12.gain, bf16[256,768]{1,0:T(8,128)(2,1)} %up_shard.1, ...), custom_call_target="tpu_custom_call" | custom-call | tf_op jit(solution)/shard_map/feed/pallas_call | solution.py:600
  174.9 19.9 %spread.1 = f32[16,16,4,128]{3,2,1,0:T(4,128)} custom-call(f32[4,128]{1,0:T(4,128)} %get-tuple-element.16.own), custom_call_target="tpu_custom_call" | custom-call | tf_op jit(solution)/shard_map/spread/pallas_call | solution.py:628
  194.7 1.5 reshape.32
  196.2 0.0 copy-start.1
  196.2 0.3 multiply_reduce_fusion
  196.5 0.1 rsqrt.11
  196.6 0.1 copy.18
  196.7 0.3 copy.19
  197.0 0.0 copy-done.2
  197.0 0.1 multiply_convert_fusion
  197.2 0.0 copy-start
  197.2 3.2 %convolution_reduce_fusion = f32[32]{0:T(128)S(1)} fusion(bf16[32,4096]{1,0:T(8,128)(2,1)S(1)} %multiply_convert_fusion, bf16[4096,512]{1,0:T(8,128)(2,1)} %param.20), kind=kOutput, calls=%fused_computation | convolution fusion | flops 134234080 | bytes 4456576 | tf_op jit(solution)/shard_map/dot_general | solution.py:643
  200.4 0.5 pad_bitcast_fusion.own
  200.9 16.7 %largest.1 = f32[1,128]{1,0:T(1,128)} custom-call(f32[1,128]{1,0:T(1,128)} %pad_bitcast_fusion.own), custom_call_target="tpu_custom_call" | custom-call | tf_op jit(solution)/shard_map/largest/pallas_call | solution.py:645
  217.6 1.1 slice_bitcast_fusion
  218.7 0.6 sqrt.7
  219.3 0.0 copy-done.1
  219.3 0.7 copy.21
  220.0 0.0 copy-done
  (2 shorter events, 0.0 us)
Async XLA Ops:
  72.4 124.6 %copy-start.2 = (bf16[4096]{0:T(1024)(128)(2,1)S(1)}, bf16[4096]{0:T(1024)(128)(2,1)}, u32[]{:S(2)}) copy-start(bf16[4096]{0:T(1024)(128)(2,1)} %param.19) | copy-start | bytes 24580
  196.2 23.1 %copy-start.1 = (bf16[256,256]{1,0:T(8,128)(2,1)S(1)}, bf16[256,256]{1,0:T(8,128)(2,1)}, u32[]{:S(2)}) copy-start(bf16[256,256]{1,0:T(8,128)(2,1)} %get-tuple-element.24) | copy-start | bytes 393220
  197.2 22.8 %copy-start = (bf16[32,4096]{1,0:T(8,128)(2,1)}, bf16[32,4096]{1,0:T(8,128)(2,1)S(1)}, u32[]{:S(2)}) copy-start(bf16[32,4096]{1,0:T(8,128)(2,1)S(1)} %multiply_convert_fusion) | copy-start | bytes 786436
